TPU v7x, 32 devices: a whole 2x2x4 slice. The times are simulated.
32 devices in a mesh: groups: 2 (over y), seq: 4 (over z), section: 2 (over x), head: 2 (over core).
Axes of the slice: x: 2, y: 2, z: 4, core: 2. Of those that a mesh axis runs over, the one named last changes fastest.
Arguments:
- queries: bfloat16 [64, 64, 128], P(('groups', 'seq'), ('section', 'head')), parts along dimension 0, may hold values from -56 to 56
- key_cache: bfloat16 [15872, 8, 128], P(('groups', 'seq'), ('section', 'head')), parts along dimension 0, may hold values from -5 to 5
- value_cache: bfloat16 [15872, 8, 128], P(('groups', 'seq'), ('section', 'head')), parts along dimension 0, may hold values from -5 to 5
- new_features: bfloat16 [512, 8192], P(('groups', 'seq')), parts along dimension 0, may hold values from -60 to 60
- key_weight: bfloat16 [8192, 1024], P('seq', ('section', 'head')), may hold values from -2 to 2
- value_weight: bfloat16 [8192, 1024], P('seq', ('section', 'head')), may hold values from -0.0625 to 0.0625
- key_gain: float32 [128], replicated, may hold values from 0.5 to 2
- out_weight: bfloat16 [8192, 8192], P(('section', 'head'), 'seq'), may hold values from -0.5 to 0.5
- frame_length: int32 [128], P('groups'), parts along dimension 0, may hold values from 1 to 256, 8192 in all
- text_frame: int32 [64], P(('groups', 'seq')), parts along dimension 0, may hold values from 0 to 63
Outputs:
- layer_output: bfloat16 [64, 8192], P(('groups', 'section', 'head'), 'seq'), parts along dimension 0
- new_keys: bfloat16 [512, 8, 128], P(('groups', 'seq'), ('section', 'head')), parts along dimension 0
- new_values: bfloat16 [512, 8, 128], P(('groups', 'seq'), ('section', 'head')), parts along dimension 0
There are 2 independent parts, one for each index of `groups`. A program takes and returns all parts, laid end to end along the dimension named above; an argument that names none is the same for every part. Nothing has to cross between parts.
Inputs may be any that keep to these rules, and one draw needn't show every extreme that they name: `frame_length`: they sum to 8192.
All inputs are finite; a program needn't handle non-finite values.
Results may differ from a plain program's by a relative error of at most 0.015.
Values may be sent and summed in bfloat16 or wider, within the bound.
No kernel may reach another device: no remote copies, remote signals or barrier semaphores. Data moves between devices by JAX's collectives and lax.ppermute only.
A program may use at most 64 MiB of HBM per device.

v0:
```python
import jax
import jax.numpy as jnp
from jax import lax
from jax.sharding import PartitionSpec as P

masked_score = -1e30
norm_epsilon = 1e-05


def for_sending(shard):

    def short(part):
        return part.astype(jnp.bfloat16) if part.dtype == jnp.float32 else part

    return jax.tree.map(short, shard)


def passed_along(shard, axis, by):
    peers = lax.axis_size(axis)
    return lax.ppermute(shard, axis, [(i, (i + by) % peers) for i in range(peers)])


def visit_block(query_block, state, key_block, value_block, key_position, score_scale):
    row_peak, row_total, row_accum, row_limit = state
    block_rows, local_heads, head_depth = query_block.shape
    local_kv = key_block.shape[1]
    grouped = query_block.reshape(block_rows, local_kv, local_heads // local_kv, head_depth)
    scores = (
        jnp.einsum("rcgd,kcd->rcgk", grouped, key_block, preferred_element_type=jnp.float32)
        * score_scale
    )
    visible = (key_position[None, :] < row_limit[:, None])[:, None, None, :]
    block_peak = jnp.max(jnp.where(visible, scores, masked_score), axis=3)
    new_peak = jnp.maximum(row_peak, block_peak)
    weights = jnp.where(visible, jnp.exp(scores - new_peak[..., None]), 0.0)
    factor = jnp.exp(row_peak - new_peak)
    row_total = factor * row_total + jnp.sum(weights, axis=3)
    update = jnp.einsum(
        "rcgk,kcd->rcgd",
        weights.astype(jnp.bfloat16),
        value_block,
        preferred_element_type=jnp.float32,
    )
    row_accum = factor[..., None] * row_accum + update
    return (new_peak, row_total, row_accum, row_limit)


def fresh_state(query_block, row_limit, local_kv):
    block_rows, local_heads, head_depth = query_block.shape
    head_shape = (block_rows, local_kv, local_heads // local_kv)
    return (
        jnp.full(head_shape, masked_score, jnp.float32),
        jnp.zeros(head_shape, jnp.float32),
        jnp.zeros(head_shape + (head_depth,), jnp.float32),
        row_limit,
    )


def pass_forward(query_block, state, with_query):
    if with_query:
        query_block = jax.tree.map(
            lambda part, own: part.astype(own.dtype),
            passed_along(for_sending(query_block), "seq", 1),
            query_block,
        )
    state = passed_along(state, "seq", 1)
    return (query_block, state)


def cycle_attend(
    blocks, move_blocks, key_block, value_block, key_position, score_scale, cycle_length
):

    def one_visit(running, with_query):
        moved_list = []
        for member, move_block in zip(running, move_blocks):
            state_now = visit_block(
                member[0], member[1], key_block, value_block, key_position, score_scale
            )
            moved_list.append(move_block(member[0], state_now, with_query))
        return tuple(moved_list)

    def two_visits(turn_index, running):
        return one_visit(one_visit(running, True), True)

    running = lax.fori_loop(0, cycle_length // 2 - 1, two_visits, blocks)
    finished = one_visit(one_visit(running, True), False)
    outputs = []
    for member in finished:
        row_peak, row_total, row_accum, row_limit = member[1]
        attended = (row_accum / row_total[..., None]).astype(jnp.bfloat16)
        outputs.append(attended.reshape(attended.shape[0], -1))
    return outputs[0]


def on_device(
    queries,
    key_cache,
    value_cache,
    new_features,
    key_weight,
    value_weight,
    key_gain,
    out_weight,
    frame_length,
    text_frame,
):
    head_depth = key_cache.shape[2]
    local_kv = key_cache.shape[1]
    kv_width = key_weight.shape[1]
    new_rows = new_features.shape[0]
    spread = lax.all_to_all(new_features, "seq", split_axis=1, concat_axis=0, tiled=True)
    stacked_weight = jnp.concatenate((key_weight, value_weight), axis=1)
    summed = lax.psum_scatter(
        jnp.dot(spread, stacked_weight, preferred_element_type=jnp.float32).astype(jnp.bfloat16),
        "seq",
        scatter_dimension=0,
        tiled=True,
    ).astype(jnp.float32)
    key_raw = summed[:, :kv_width]
    value_raw = summed[:, kv_width:]
    key_heads = key_raw.reshape(new_rows, local_kv, head_depth)
    mean_square = jnp.mean(key_heads * key_heads, axis=2, keepdims=True)
    new_keys = (key_heads * lax.rsqrt(mean_square + norm_epsilon) * key_gain).astype(jnp.bfloat16)
    new_values = value_raw.reshape(new_rows, local_kv, head_depth).astype(jnp.bfloat16)
    key_block = jnp.concatenate((key_cache, new_keys), axis=0)
    value_block = jnp.concatenate((value_cache, new_values), axis=0)
    block_keys = key_block.shape[0]
    key_position = (
        lax.axis_index("seq") * block_keys + jnp.arange(block_keys, dtype=jnp.int32)
    ).astype(jnp.float32)
    frame_index = jnp.arange(frame_length.shape[0], dtype=jnp.int32)
    row_limit = jnp.sum(
        jnp.where(frame_index[None, :] <= text_frame[:, None], frame_length[None, :], 0), axis=1
    ).astype(jnp.float32)
    score_scale = head_depth ** (-0.5)
    cycle_length = lax.axis_size("seq")
    blocks = ((queries, fresh_state(queries, row_limit, local_kv)),)
    attended = cycle_attend(
        blocks, (pass_forward,), key_block, value_block, key_position, score_scale, cycle_length
    )
    partial_terms = jnp.dot(
        lax.all_gather(attended, "seq", axis=0, tiled=True),
        out_weight,
        preferred_element_type=jnp.float32,
    )
    layer_output = lax.psum_scatter(
        partial_terms.astype(jnp.bfloat16), ("section", "head"), scatter_dimension=0, tiled=True
    )
    return (layer_output, new_keys, new_values)


def solution(mesh):
    placed = (
        P(("groups", "seq"), ("section", "head"), None),
        P(("groups", "seq"), ("section", "head"), None),
        P(("groups", "seq"), ("section", "head"), None),
        P(("groups", "seq"), None),
        P("seq", ("section", "head")),
        P("seq", ("section", "head")),
        P(),
        P(("section", "head"), "seq"),
        P("groups"),
        P(("groups", "seq")),
    )
    return jax.shard_map(
        on_device,
        mesh=mesh,
        in_specs=placed,
        out_specs=(
            P(("groups", "section", "head"), "seq"),
            P(("groups", "seq"), ("section", "head"), None),
            P(("groups", "seq"), ("section", "head"), None),
        ),
        check_vma=False,
    )
```

profile of v0, /device:TPU:0, one launch (start us, length us, event | category | flops | bytes accessed | tf_op | source)
XLA Modules:
  0.0 143.7 jit_solution(10098577655566775212)
XLA Ops:
  7.2 2.3 %copy.138 = bf16[8,4,8,2048]{3,2,0,1:T(8,128)(2,1)} copy(bf16[8,4,8,2048]{3,2,1,0:T(8,128)(2,1)} %bitcast.94) | data formatting | bytes 2097152 | tf_op jit(solution)/shard_map/all_to_all | solution.py:112
  9.5 6.3 %all-to-all-start = ((bf16[64,4,2048]{2,0,1:T(8,128)(2,1)}), bf16[64,4,2048]{2,0,1:T(8,128)(2,1)S(1)}, u32[]{:S(2)}, u32[]{:S(2)}) async-start(bf16[64,4,2048]{2,0,1:T(8,128)(2,1)} %bitcast.90), calls=%async_computation | async-start | bytes 2097152 | tf_op jit(solution)/shard_map/all_to_all | solution.py:112
  16.1 2.1 %collective-permute-start.1 = (f32[8]{0:T(128)S(1)}, f32[8]{0:T(128)S(1)}, u32[]{:S(2)}, u32[]{:S(2)}) collective-permute-start(f32[8]{0:T(128)S(1)} %convert_element_type.49), channel_id=1, source_target_pairs={{0,4},{4,8},{8,12},{12,0},{1,5},{5,9},{9,13},{13,1},{2,6},{6,10},{... | collective-permute-start | bytes 104 | tf_op jit(solution)/shard_map/while/body/eval_jaxpr/ppermute | solution.py:20
  18.1 1.5 %collective-permute-start.2 = (bf16[8,16,128]{2,1,0:T(8,128)(2,1)S(1)}, bf16[8,16,128]{2,1,0:T(8,128)(2,1)S(1)}, u32[]{:S(2)}, u32[]{:S(2)}) collective-permute-start(bf16[8,16,128]{2,1,0:T(8,128)(2,1)S(1)} %copy-done.3), channel_id=1, source_target_pairs={{0,4},{4,8},{8,12},{12,0},{1,5},{5,9},{9,13},{13,1},{2,6},{6,10},{... | collective-permute-start | bytes 98312 | tf_op jit(solution)/shard_map/while/body/eval_jaxpr/ppermute | solution.py:20
  19.6 22.7 %all-to-all-done = bf16[64,4,2048]{2,0,1:T(8,128)(2,1)S(1)} async-done(((bf16[64,4,2048]{2,0,1:T(8,128)(2,1)}), bf16[64,4,2048]{2,0,1:T(8,128)(2,1)S(1)}, u32[]{:S(2)}, u32[]{:S(2)}) %all-to-all-start) | async-done | bytes 1048608 | tf_op jit(solution)/shard_map/all_to_all | solution.py:112
  42.3 2.4 %fusion.11 = bf16[256,512]{0,1:T(8,128)(2,1)S(1)} fusion(bf16[256,2048]{1,0:T(8,128)(2,1)S(1)} %bitcast.95, bf16[2048,256]{1,0:T(8,128)(2,1)} %param.15, bf16[2048,256]{1,0:T(8,128)(2,1)} %param.14), kind=kOutput, calls=%fused_computation.14 | convolution fusion | flops 541196288 | bytes 3407872 | tf_op jit(solution)/shard_map/dot_general | solution.py:115
  44.7 0.8 copy.112
  46.2 5.4 %collective-permute-done.4 = f32[8]{0:T(128)S(1)} collective-permute-done((f32[8]{0:T(128)S(1)}, f32[8]{0:T(128)S(1)}, u32[]{:S(2)}, u32[]{:S(2)}) %collective-permute-start.4) | collective-permute-done | bytes 64 | tf_op jit(solution)/shard_map/while/body/eval_jaxpr/ppermute | solution.py:20
  51.6 5.4 %collective-permute-done.7 = f32[8]{0:T(128)S(1)} collective-permute-done((f32[8]{0:T(128)S(1)}, f32[8]{0:T(128)S(1)}, u32[]{:S(2)}, u32[]{:S(2)}) %collective-permute-start.7) | collective-permute-done | bytes 64 | tf_op jit(solution)/shard_map/ppermute | solution.py:20
  57.0 0.5 collective-permute-done.5
  57.5 7.0 %reduce-scatter.7.cloned.1.call-done = bf16[64,512]{1,0:T(8,128)(2,1)} async-done(((bf16[256,512]{1,0:T(8,128)(2,1)}), bf16[64,512]{1,0:T(8,128)(2,1)}) %reduce-scatter.7.cloned.1.call-update) | async-done | bytes 65552 | tf_op jit(solution)/shard_map/reduce_scatter | solution.py:114
  64.5 0.8 fusion.58
  65.6 0.6 select_reduce_fusion.3
  67.3 1.3 collective-permute-start.9
  68.6 0.5 collective-permute-start.13
  69.1 0.6 select_reduce_fusion.2
  69.7 0.6 select_reduce_fusion.1
  70.3 0.6 select_reduce_fusion
  70.9 0.9 collective-permute-done
  71.7 2.4 %collective-permute-start.3 = (f32[8,2,8]{2,0,1:T(8,128)S(1)}, f32[8,2,8]{2,0,1:T(8,128)S(1)}, u32[]{:S(2)}, u32[]{:S(2)}) collective-permute-start(f32[8,2,8]{2,0,1:T(8,128)S(1)} %max.22), channel_id=1, source_target_pairs={{0,4},{4,8},{8,12},{12,0},{1,5},{5,9},{9,13},{13,1},{2,6},{6,10},{... | collective-permute-start | bytes 1544 | tf_op jit(solution)/shard_map/while/body/eval_jaxpr/ppermute | solution.py:20
  74.6 2.6 %collective-permute-done.3 = f32[8,2,8]{2,0,1:T(8,128)S(1)} collective-permute-done((f32[8,2,8]{2,0,1:T(8,128)S(1)}, f32[8,2,8]{2,0,1:T(8,128)S(1)}, u32[]{:S(2)}, u32[]{:S(2)}) %collective-permute-start.3) | collective-permute-done | bytes 544 | tf_op jit(solution)/shard_map/while/body/eval_jaxpr/ppermute | solution.py:20
  77.2 0.6 collective-permute-start.6
  78.1 1.9 %collective-permute-done.14 = f32[8,2,8]{2,0,1:T(8,128)S(1)} collective-permute-done((f32[8,2,8]{2,0,1:T(8,128)S(1)}, f32[8,2,8]{2,0,1:T(8,128)S(1)}, u32[]{:S(2)}, u32[]{:S(2)}) %collective-permute-start.14) | collective-permute-done | bytes 544 | tf_op jit(solution)/shard_map/while/body/eval_jaxpr/ppermute | solution.py:20
  80.0 2.7 %collective-permute-done.6 = f32[8,2,8]{2,0,1:T(8,128)S(1)} collective-permute-done((f32[8,2,8]{2,0,1:T(8,128)S(1)}, f32[8,2,8]{2,0,1:T(8,128)S(1)}, u32[]{:S(2)}, u32[]{:S(2)}) %collective-permute-start.6) | collective-permute-done | bytes 544 | tf_op jit(solution)/shard_map/ppermute | solution.py:20
  83.6 5.7 %collective-permute-done.10 = f32[8,2,8,128]{3,2,0,1:T(8,128)S(1)} collective-permute-done((f32[8,2,8,128]{3,2,0,1:T(8,128)S(1)}, f32[8,2,8,128]{3,2,0,1:T(8,128)S(1)}, u32[]{:S(2)}, u32[]{:S(2)}) %collective-permute-start.10) | collective-permute-done | bytes 65568 | tf_op jit(solution)/shard_map/while/body/eval_jaxpr/ppermute | solution.py:20
  89.8 6.0 %collective-permute-done.11 = f32[8,2,8,128]{3,2,0,1:T(8,128)S(1)} collective-permute-done((f32[8,2,8,128]{3,2,0,1:T(8,128)S(1)}, f32[8,2,8,128]{3,2,0,1:T(8,128)S(1)}, u32[]{:S(2)}, u32[]{:S(2)}) %collective-permute-start.11) | collective-permute-done | bytes 65568 | tf_op jit(solution)/shard_map/ppermute | solution.py:20
  96.3 6.1 %collective-permute-done.16 = f32[8,2,8]{2,0,1:T(8,128)S(1)} collective-permute-done((f32[8,2,8]{2,0,1:T(8,128)S(1)}, f32[8,2,8]{2,0,1:T(8,128)S(1)}, u32[]{:S(2)}, u32[]{:S(2)}) %collective-permute-start.16) | collective-permute-done | bytes 544 | tf_op jit(solution)/shard_map/ppermute | solution.py:20
  102.6 13.3 %all_gather.3 = bf16[32,2048]{1,0:T(8,128)(2,1)S(1)} all-gather(bf16[8,2048]{1,0:T(8,128)(2,1)S(1)} %bitcast.98), channel_id=1, replica_groups=mesh['groups'=2,'seq'=4,'section'=2,'head'=2] {'seq'}, dimensions={0}, use_global_device_ids=true | all-gather | bytes 163840 | tf_op jit(solution)/shard_map/all_gather | solution.py:143
  115.9 2.2 %convolution_convert_fusion = bf16[32,2048]{1,0:T(8,128)(2,1)} fusion(bf16[32,2048]{1,0:T(8,128)(2,1)S(1)} %all_gather.3, bf16[2048,2048]{1,0:T(8,128)(2,1)S(1)} %bitcast.93), kind=kOutput, calls=%fused_computation.8 | convolution fusion | flops 268500992 | bytes 8650752 | tf_op jit(solution)/shard_map/dot_general | solution.py:142
  118.1 0.6 copy.107
  118.8 0.7 copy.110
  119.5 17.3 %reduce-scatter.5.cloned.1.call-done = bf16[8,2048]{1,0:T(8,128)(2,1)} async-done(((bf16[32,2048]{1,0:T(8,128)(2,1)}), bf16[8,2048]{1,0:T(8,128)(2,1)}) %reduce-scatter.5.cloned.1.call-update) | async-done | bytes 32784 | tf_op jit(solution)/shard_map/reduce_scatter | solution.py:147
  (70 shorter events, 5.3 us)
Async XLA Ops:
  7.2 8.7 %copy-start.4 = (s32[64]{0:T(128)S(1)}, s32[64]{0:T(128)}, u32[]{:S(2)}) copy-start(s32[64]{0:T(128)} %param.18) | copy-start | bytes 772
  7.2 8.7 %copy-start.5 = (s32[8]{0:T(128)S(1)}, s32[8]{0:T(128)}, u32[]{:S(2)}) copy-start(s32[8]{0:T(128)} %param.19) | copy-start | bytes 100
  7.2 10.9 %copy-start.3 = (bf16[8,16,128]{2,1,0:T(8,128)(2,1)S(1)}, bf16[8,16,128]{2,1,0:T(8,128)(2,1)}, u32[]{:S(2)}) copy-start(bf16[8,16,128]{2,1,0:T(8,128)(2,1)} %param.10) | copy-start | bytes 98308
  9.5 32.8 %all-to-all-start = ((bf16[64,4,2048]{2,0,1:T(8,128)(2,1)}), bf16[64,4,2048]{2,0,1:T(8,128)(2,1)S(1)}, u32[]{:S(2)}, u32[]{:S(2)}) async-start(bf16[64,4,2048]{2,0,1:T(8,128)(2,1)} %bitcast.90), calls=%async_computation | async-start | bytes 2097152 | tf_op jit(solution)/shard_map/all_to_all | solution.py:112
  15.9 48.6 %reduce-scatter.7.cloned.1.call-start = ((), (), s32[]{:S(2)}) async-start(), calls=%async_computation.4 | async-start | bytes 327680 | tf_op jit(solution)/shard_map/reduce_scatter | solution.py:114
  16.1 30.1 %collective-permute-start.1 = (f32[8]{0:T(128)S(1)}, f32[8]{0:T(128)S(1)}, u32[]{:S(2)}, u32[]{:S(2)}) collective-permute-start(f32[8]{0:T(128)S(1)} %convert_element_type.49), channel_id=1, source_target_pairs={{0,4},{4,8},{8,12},{12,0},{1,5},{5,9},{9,13},{13,1},{2,6},{6,10},{... | collective-permute-start | bytes 104 | tf_op jit(solution)/shard_map/while/body/eval_jaxpr/ppermute | solution.py:20
  18.1 33.4 %collective-permute-start.2 = (bf16[8,16,128]{2,1,0:T(8,128)(2,1)S(1)}, bf16[8,16,128]{2,1,0:T(8,128)(2,1)S(1)}, u32[]{:S(2)}, u32[]{:S(2)}) collective-permute-start(bf16[8,16,128]{2,1,0:T(8,128)(2,1)S(1)} %copy-done.3), channel_id=1, source_target_pairs={{0,4},{4,8},{8,12},{12,0},{1,5},{5,9},{9,13},{13,1},{2,6},{6,10},{... | collective-permute-start | bytes 98312 | tf_op jit(solution)/shard_map/while/body/eval_jaxpr/ppermute | solution.py:20
  42.3 3.3 %copy-start = (bf16[1984,2,128]{2,1,0:T(2,128)(2,1)S(1)}, bf16[1984,2,128]{2,1,0:T(2,128)(2,1)}, u32[]{:S(2)}) copy-start(bf16[1984,2,128]{2,1,0:T(2,128)(2,1)} %param.11) | copy-start | bytes 3047428
  44.7 1.3 copy-start.1
  45.6 91.3 %reduce-scatter.5.cloned.1.call-start = ((), (), s32[]{:S(2)}) async-start(), calls=%async_computation.3 | async-start | bytes 163840 | tf_op jit(solution)/shard_map/reduce_scatter | solution.py:147
  45.6 19.9 %copy-start.2 = (f32[128]{0:T(128)S(1)}, f32[128]{0:T(128)}, u32[]{:S(2)}) copy-start(f32[128]{0:T(128)} %param.16) | copy-start | bytes 1540
  46.1 5.4 %collective-permute-start.4 = (f32[8]{0:T(128)S(1)}, f32[8]{0:T(128)S(1)}, u32[]{:S(2)}, u32[]{:S(2)}) collective-permute-start(f32[8]{0:T(128)S(1)} %collective-permute-done.1), channel_id=1, source_target_pairs={{0,4},{4,8},{8,12},{12,0},{1,5},{5,9},{9,13},{13,1},{2,6},{6,10},{... | collective-permute-start | bytes 104 | tf_op jit(solution)/shard_map/while/body/eval_jaxpr/ppermute | solution.py:20
  51.6 5.4 %collective-permute-start.7 = (f32[8]{0:T(128)S(1)}, f32[8]{0:T(128)S(1)}, u32[]{:S(2)}, u32[]{:S(2)}) collective-permute-start(f32[8]{0:T(128)S(1)} %collective-permute-done.4), channel_id=1, source_target_pairs={{0,4},{4,8},{8,12},{12,0},{1,5},{5,9},{9,13},{13,1},{2,6},{6,10},{... | collective-permute-start | bytes 104 | tf_op jit(solution)/shard_map/ppermute | solution.py:20
  51.6 5.9 %collective-permute-start.5 = (bf16[8,16,128]{2,1,0:T(8,128)(2,1)S(1)}, bf16[8,16,128]{2,1,0:T(8,128)(2,1)S(1)}, u32[]{:S(2)}, u32[]{:S(2)}) collective-permute-start(bf16[8,16,128]{2,1,0:T(8,128)(2,1)S(1)} %collective-permute-done.2), channel_id=1, source_target_pairs={{0,4},{4,8},{8,12},{12,0},{1,5},{5,9},{9,13},{13,1},{2,6},{6,10},{... | collective-permute-start | bytes 98312 | tf_op jit(solution)/shard_map/while/body/eval_jaxpr/ppermute | solution.py:20
  57.5 12.8 %collective-permute-start.8 = (bf16[8,16,128]{2,1,0:T(8,128)(2,1)S(1)}, bf16[8,16,128]{2,1,0:T(8,128)(2,1)S(1)}, u32[]{:S(2)}, u32[]{:S(2)}) collective-permute-start(bf16[8,16,128]{2,1,0:T(8,128)(2,1)S(1)} %collective-permute-done.5), channel_id=1, source_target_pairs={{0,4},{4,8},{8,12},{12,0},{1,5},{5,9},{9,13},{13,1},{2,6},{6,10},{... | collective-permute-start | bytes 98312 | tf_op jit(solution)/shard_map/ppermute | solution.py:20
  66.2 5.5 %collective-permute-start = (f32[8,2,8]{2,0,1:T(8,128)S(1)}, f32[8,2,8]{2,0,1:T(8,128)S(1)}, u32[]{:S(2)}, u32[]{:S(2)}) collective-permute-start(f32[8,2,8]{2,0,1:T(8,128)S(1)} %broadcast_maximum_fusion), channel_id=1, source_target_pairs={{0,4},{4,8},{8,12},{12,0},{1,5},{5,9},{9,13},{13,1},{2,6},{6,10},{... | collective-permute-start | bytes 1544 | tf_op jit(solution)/shard_map/while/body/eval_jaxpr/ppermute | solution.py:20
  67.3 15.4 %collective-permute-start.9 = (f32[8,2,8,128]{3,2,0,1:T(8,128)S(1)}, f32[8,2,8,128]{3,2,0,1:T(8,128)S(1)}, u32[]{:S(2)}, u32[]{:S(2)}) collective-permute-start(f32[8,2,8,128]{3,2,0,1:T(8,128)S(1)} %fusion.14), channel_id=1, source_target_pairs={{0,4},{4,8},{8,12},{12,0},{1,5},{5,9},{9,13},{13,1},{2,6},{6,10},{... | collective-permute-start | bytes 196616 | tf_op jit(solution)/shard_map/while/body/eval_jaxpr/ppermute | solution.py:20
  68.6 5.8 %collective-permute-start.13 = (f32[8,2,8]{2,0,1:T(8,128)S(1)}, f32[8,2,8]{2,0,1:T(8,128)S(1)}, u32[]{:S(2)}, u32[]{:S(2)}) collective-permute-start(f32[8,2,8]{2,0,1:T(8,128)S(1)} %get-tuple-element.67), channel_id=1, source_target_pairs={{0,4},{4,8},{8,12},{12,0},{1,5},{5,9},{9,13},{13,1},{2,6},{6,10},{... | collective-permute-start | bytes 1544 | tf_op jit(solution)/shard_map/while/body/eval_jaxpr/ppermute | solution.py:20
  71.7 5.4 %collective-permute-start.3 = (f32[8,2,8]{2,0,1:T(8,128)S(1)}, f32[8,2,8]{2,0,1:T(8,128)S(1)}, u32[]{:S(2)}, u32[]{:S(2)}) collective-permute-start(f32[8,2,8]{2,0,1:T(8,128)S(1)} %max.22), channel_id=1, source_target_pairs={{0,4},{4,8},{8,12},{12,0},{1,5},{5,9},{9,13},{13,1},{2,6},{6,10},{... | collective-permute-start | bytes 1544 | tf_op jit(solution)/shard_map/while/body/eval_jaxpr/ppermute | solution.py:20
  74.5 5.5 %collective-permute-start.14 = (f32[8,2,8]{2,0,1:T(8,128)S(1)}, f32[8,2,8]{2,0,1:T(8,128)S(1)}, u32[]{:S(2)}, u32[]{:S(2)}) collective-permute-start(f32[8,2,8]{2,0,1:T(8,128)S(1)} %get-tuple-element.58), channel_id=1, source_target_pairs={{0,4},{4,8},{8,12},{12,0},{1,5},{5,9},{9,13},{13,1},{2,6},{6,10},{... | collective-permute-start | bytes 1544 | tf_op jit(solution)/shard_map/while/body/eval_jaxpr/ppermute | solution.py:20
  77.2 5.5 %collective-permute-start.6 = (f32[8,2,8]{2,0,1:T(8,128)S(1)}, f32[8,2,8]{2,0,1:T(8,128)S(1)}, u32[]{:S(2)}, u32[]{:S(2)}) collective-permute-start(f32[8,2,8]{2,0,1:T(8,128)S(1)} %max.23), channel_id=1, source_target_pairs={{0,4},{4,8},{8,12},{12,0},{1,5},{5,9},{9,13},{13,1},{2,6},{6,10},{... | collective-permute-start | bytes 1544 | tf_op jit(solution)/shard_map/ppermute | solution.py:20
  80.0 9.8 %collective-permute-start.15 = (f32[8,2,8]{2,0,1:T(8,128)S(1)}, f32[8,2,8]{2,0,1:T(8,128)S(1)}, u32[]{:S(2)}, u32[]{:S(2)}) collective-permute-start(f32[8,2,8]{2,0,1:T(8,128)S(1)} %get-tuple-element.56), channel_id=1, source_target_pairs={{0,4},{4,8},{8,12},{12,0},{1,5},{5,9},{9,13},{13,1},{2,6},{6,10},{... | collective-permute-start | bytes 1544 | tf_op jit(solution)/shard_map/ppermute | solution.py:20
  83.1 6.1 %collective-permute-start.10 = (f32[8,2,8,128]{3,2,0,1:T(8,128)S(1)}, f32[8,2,8,128]{3,2,0,1:T(8,128)S(1)}, u32[]{:S(2)}, u32[]{:S(2)}) collective-permute-start(f32[8,2,8,128]{3,2,0,1:T(8,128)S(1)} %multiply_add_fusion.2), channel_id=1, source_target_pairs={{0,4},{4,8},{8,12},{12,0},{1,5},{5,9},{9,13},{13,1},{2,6},{6,10},{... | collective-permute-start | bytes 196616 | tf_op jit(solution)/shard_map/while/body/eval_jaxpr/ppermute | solution.py:20
  83.2 32.7 %slice-start = ((s8[8388608]{0:T(1024)(128)(4,1)}), s8[4194304]{0:T(1024)(128)(4,1)S(1)}, s32[]{:S(2)}) async-start(s8[8388608]{0:T(1024)(128)(4,1)} %bitcast.92), calls=%async_computation.5 | async-start | bytes 8388608
  89.2 26.7 %slice-start.1 = ((s8[8388608]{0:T(1024)(128)(4,1)}), s8[4194304]{0:T(1024)(128)(4,1)S(1)}, s32[]{:S(2)}) async-start(s8[8388608]{0:T(1024)(128)(4,1)} %bitcast.92), calls=%async_computation.6 | async-start | bytes 8388608
  89.7 6.1 %collective-permute-start.11 = (f32[8,2,8,128]{3,2,0,1:T(8,128)S(1)}, f32[8,2,8,128]{3,2,0,1:T(8,128)S(1)}, u32[]{:S(2)}, u32[]{:S(2)}) collective-permute-start(f32[8,2,8,128]{3,2,0,1:T(8,128)S(1)} %multiply_add_fusion.1), channel_id=1, source_target_pairs={{0,4},{4,8},{8,12},{12,0},{1,5},{5,9},{9,13},{13,1},{2,6},{6,10},{... | collective-permute-start | bytes 196616 | tf_op jit(solution)/shard_map/ppermute | solution.py:20
  96.2 6.2 %collective-permute-start.12 = (f32[8,2,8,128]{3,2,0,1:T(8,128)S(1)}, f32[8,2,8,128]{3,2,0,1:T(8,128)S(1)}, u32[]{:S(2)}, u32[]{:S(2)}) collective-permute-start(f32[8,2,8,128]{3,2,0,1:T(8,128)S(1)} %multiply_add_fusion), channel_id=1, source_target_pairs={{0,4},{4,8},{8,12},{12,0},{1,5},{5,9},{9,13},{13,1},{2,6},{6,10},{... | collective-permute-start | bytes 196616 | tf_op jit(solution)/shard_map/ppermute | solution.py:20
  96.3 6.2 %collective-permute-start.16 = (f32[8,2,8]{2,0,1:T(8,128)S(1)}, f32[8,2,8]{2,0,1:T(8,128)S(1)}, u32[]{:S(2)}, u32[]{:S(2)}) collective-permute-start(f32[8,2,8]{2,0,1:T(8,128)S(1)} %get-tuple-element.54), channel_id=1, source_target_pairs={{0,4},{4,8},{8,12},{12,0},{1,5},{5,9},{9,13},{13,1},{2,6},{6,10},{... | collective-permute-start | bytes 1544 | tf_op jit(solution)/shard_map/ppermute | solution.py:20
Sparse Core Ops, SparseCore 0:
  45.7 18.7 reduce-scatter.6
  118.3 18.5 reduce-scatter.4
where the time goes:
time: 144 us
  waiting for transfers between devices  84 us (58%)
  starting transfers between devices  15.2 us (11%)
  between operations  14.3 us (10%)
  blocking collectives  13.3 us (9%)
  matrix products  8.47 us (6%)
  local copies, waits for them, and re-layouts  5.37 us (4%)
  other arithmetic  2.99 us (2%)
    ppermute x17, waiting for transfers between devices, passed_along(): lax.ppermute(shard, axis, [(i, (i + by) % peers) for i in range(peers)])  36.9 us
    all_to_all x1, waiting for transfers between devices, on_device(): lax.all_to_all(new_features, 'seq', split_axis=1, concat_axis=0, tiled=True)  22.7 us
    reduce_scatter x1, waiting for transfers between devices, on_device(): lax.psum_scatter(partial_terms.astype(jnp.bfloat16), ('section', 'head'),...  17.3 us
    all_gather x1, blocking collectives, on_device(): lax.all_gather(attended, 'seq', axis=0, tiled=True)  13.3 us
    ppermute x17, starting transfers between devices, passed_along(): lax.ppermute(shard, axis, [(i, (i + by) % peers) for i in range(peers)])  8.83 us
    reduce_scatter x1, waiting for transfers between devices, on_device(): lax.psum_scatter(jnp.dot(spread, stacked_weight, preferred_element_type=j...  6.96 us
    all_to_all x1, starting transfers between devices, on_device(): lax.all_to_all(new_features, 'seq', split_axis=1, concat_axis=0, tiled=True)  6.35 us
  transfers between devices with their start and end apart: 20, of which 13 were waited for; matrix products, arithmetic and copies ran while one was open for 8% of the time, Pallas kernels for 0%

commit v1 on v0

--- a/solution.py
+++ b/solution.py
@@ -140,7 +140,9 @@
         blocks, (pass_forward,), key_block, value_block, key_position, score_scale, cycle_length
     )
     partial_terms = jnp.dot(
-        lax.all_gather(attended, "seq", axis=0, tiled=True),
+        jnp.concatenate(
+            lax.all_to_all(jnp.stack([attended] * lax.axis_size("seq")), "seq", 0, 0), axis=0
+        ),
         out_weight,
         preferred_element_type=jnp.float32,
     )

time: 144 us -> 139 us (0.965)
  blocking collectives: 13.3 us -> 8.31 us
    all_gather x1 -> x0, blocking collectives: 13.3 us -> none  [on_device(): lax.all_gather(attended, 'seq', axis=0, tiled=True)]
    all_to_all x0 -> x1, blocking collectives: none -> 8.31 us  [on_device(): lax.all_to_all(jnp.stack([attended] * lax.axis_size('seq')), 'seq', 0, 0)]
where the time goes in v1:
time: 139 us
  waiting for transfers between devices  84 us (60%)
  starting transfers between devices  15.2 us (11%)
  between operations  14.3 us (10%)
  matrix products  8.47 us (6%)
  blocking collectives  8.31 us (6%)
  local copies, waits for them, and re-layouts  5.38 us (4%)
  other arithmetic  2.99 us (2%)
    ppermute x17, waiting for transfers between devices, passed_along(): lax.ppermute(shard, axis, [(i, (i + by) % peers) for i in range(peers)])  37.1 us
    all_to_all x1, waiting for transfers between devices, on_device(): lax.all_to_all(new_features, 'seq', split_axis=1, concat_axis=0, tiled=True)  22.7 us
    reduce_scatter x1, waiting for transfers between devices, on_device(): lax.psum_scatter(partial_terms.astype(jnp.bfloat16), ('section', 'head'),...  17.2 us
    ppermute x17, starting transfers between devices, passed_along(): lax.ppermute(shard, axis, [(i, (i + by) % peers) for i in range(peers)])  8.83 us
    all_to_all x1, blocking collectives, on_device(): lax.all_to_all(jnp.stack([attended] * lax.axis_size('seq')), 'seq', 0, 0)  8.31 us
    reduce_scatter x1, waiting for transfers between devices, on_device(): lax.psum_scatter(jnp.dot(spread, stacked_weight, preferred_element_type=j...  6.96 us
    all_to_all x1, starting transfers between devices, on_device(): lax.all_to_all(new_features, 'seq', split_axis=1, concat_axis=0, tiled=True)  6.35 us
  transfers between devices with their start and end apart: 20, of which 13 were waited for; matrix products, arithmetic and copies ran while one was open for 8% of the time, Pallas kernels for 0%

profile of v1, /device:TPU:0, one launch (start us, length us, event | category | flops | bytes accessed | tf_op | source)
XLA Modules:
  0.0 138.7 jit_solution(10752726882065782231)
XLA Ops:
  7.2 2.3 %copy.138 = bf16[8,4,8,2048]{3,2,0,1:T(8,128)(2,1)} copy(bf16[8,4,8,2048]{3,2,1,0:T(8,128)(2,1)} %bitcast.96) | data formatting | bytes 2097152 | tf_op jit(solution)/shard_map/all_to_all | solution.py:112
  9.5 6.3 %all-to-all-start = ((bf16[64,4,2048]{2,0,1:T(8,128)(2,1)}), bf16[64,4,2048]{2,0,1:T(8,128)(2,1)S(1)}, u32[]{:S(2)}, u32[]{:S(2)}) async-start(bf16[64,4,2048]{2,0,1:T(8,128)(2,1)} %bitcast.92), calls=%async_computation | async-start | bytes 2097152 | tf_op jit(solution)/shard_map/all_to_all | solution.py:112
  16.1 2.1 %collective-permute-start.1 = (f32[8]{0:T(128)S(1)}, f32[8]{0:T(128)S(1)}, u32[]{:S(2)}, u32[]{:S(2)}) collective-permute-start(f32[8]{0:T(128)S(1)} %convert_element_type.49), channel_id=1, source_target_pairs={{0,4},{4,8},{8,12},{12,0},{1,5},{5,9},{9,13},{13,1},{2,6},{6,10},{... | collective-permute-start | bytes 104 | tf_op jit(solution)/shard_map/while/body/eval_jaxpr/ppermute | solution.py:20
  18.1 1.5 %collective-permute-start.2 = (bf16[8,16,128]{2,1,0:T(8,128)(2,1)S(1)}, bf16[8,16,128]{2,1,0:T(8,128)(2,1)S(1)}, u32[]{:S(2)}, u32[]{:S(2)}) collective-permute-start(bf16[8,16,128]{2,1,0:T(8,128)(2,1)S(1)} %copy-done.3), channel_id=1, source_target_pairs={{0,4},{4,8},{8,12},{12,0},{1,5},{5,9},{9,13},{13,1},{2,6},{6,10},{... | collective-permute-start | bytes 98312 | tf_op jit(solution)/shard_map/while/body/eval_jaxpr/ppermute | solution.py:20
  19.6 22.7 %all-to-all-done = bf16[64,4,2048]{2,0,1:T(8,128)(2,1)S(1)} async-done(((bf16[64,4,2048]{2,0,1:T(8,128)(2,1)}), bf16[64,4,2048]{2,0,1:T(8,128)(2,1)S(1)}, u32[]{:S(2)}, u32[]{:S(2)}) %all-to-all-start) | async-done | bytes 1048608 | tf_op jit(solution)/shard_map/all_to_all | solution.py:112
  42.3 2.4 %fusion.11 = bf16[256,512]{0,1:T(8,128)(2,1)S(1)} fusion(bf16[256,2048]{1,0:T(8,128)(2,1)S(1)} %bitcast.97, bf16[2048,256]{1,0:T(8,128)(2,1)} %param.15, bf16[2048,256]{1,0:T(8,128)(2,1)} %param.14), kind=kOutput, calls=%fused_computation.14 | convolution fusion | flops 541196288 | bytes 3407872 | tf_op jit(solution)/shard_map/dot_general | solution.py:115
  44.7 0.8 copy.112
  46.2 5.4 %collective-permute-done.4 = f32[8]{0:T(128)S(1)} collective-permute-done((f32[8]{0:T(128)S(1)}, f32[8]{0:T(128)S(1)}, u32[]{:S(2)}, u32[]{:S(2)}) %collective-permute-start.4) | collective-permute-done | bytes 64 | tf_op jit(solution)/shard_map/while/body/eval_jaxpr/ppermute | solution.py:20
  51.6 5.4 %collective-permute-done.7 = f32[8]{0:T(128)S(1)} collective-permute-done((f32[8]{0:T(128)S(1)}, f32[8]{0:T(128)S(1)}, u32[]{:S(2)}, u32[]{:S(2)}) %collective-permute-start.7) | collective-permute-done | bytes 64 | tf_op jit(solution)/shard_map/ppermute | solution.py:20
  57.0 0.5 collective-permute-done.5
  57.5 7.0 %reduce-scatter.7.cloned.1.call-done = bf16[64,512]{1,0:T(8,128)(2,1)} async-done(((bf16[256,512]{1,0:T(8,128)(2,1)}), bf16[64,512]{1,0:T(8,128)(2,1)}) %reduce-scatter.7.cloned.1.call-update) | async-done | bytes 65552 | tf_op jit(solution)/shard_map/reduce_scatter | solution.py:114
  64.5 0.8 fusion.59
  65.6 0.6 select_reduce_fusion.3
  67.3 1.3 collective-permute-start.9
  68.6 0.5 collective-permute-start.13
  69.1 0.6 select_reduce_fusion.2
  69.7 0.6 select_reduce_fusion.1
  70.3 0.6 select_reduce_fusion
  70.9 0.9 collective-permute-done
  71.7 2.4 %collective-permute-start.3 = (f32[8,2,8]{2,0,1:T(8,128)S(1)}, f32[8,2,8]{2,0,1:T(8,128)S(1)}, u32[]{:S(2)}, u32[]{:S(2)}) collective-permute-start(f32[8,2,8]{2,0,1:T(8,128)S(1)} %max.22), channel_id=1, source_target_pairs={{0,4},{4,8},{8,12},{12,0},{1,5},{5,9},{9,13},{13,1},{2,6},{6,10},{... | collective-permute-start | bytes 1544 | tf_op jit(solution)/shard_map/while/body/eval_jaxpr/ppermute | solution.py:20
  74.6 2.6 %collective-permute-done.3 = f32[8,2,8]{2,0,1:T(8,128)S(1)} collective-permute-done((f32[8,2,8]{2,0,1:T(8,128)S(1)}, f32[8,2,8]{2,0,1:T(8,128)S(1)}, u32[]{:S(2)}, u32[]{:S(2)}) %collective-permute-start.3) | collective-permute-done | bytes 544 | tf_op jit(solution)/shard_map/while/body/eval_jaxpr/ppermute | solution.py:20
  77.2 0.6 collective-permute-start.6
  78.1 1.9 %collective-permute-done.14 = f32[8,2,8]{2,0,1:T(8,128)S(1)} collective-permute-done((f32[8,2,8]{2,0,1:T(8,128)S(1)}, f32[8,2,8]{2,0,1:T(8,128)S(1)}, u32[]{:S(2)}, u32[]{:S(2)}) %collective-permute-start.14) | collective-permute-done | bytes 544 | tf_op jit(solution)/shard_map/while/body/eval_jaxpr/ppermute | solution.py:20
  80.0 2.7 %collective-permute-done.6 = f32[8,2,8]{2,0,1:T(8,128)S(1)} collective-permute-done((f32[8,2,8]{2,0,1:T(8,128)S(1)}, f32[8,2,8]{2,0,1:T(8,128)S(1)}, u32[]{:S(2)}, u32[]{:S(2)}) %collective-permute-start.6) | collective-permute-done | bytes 544 | tf_op jit(solution)/shard_map/ppermute | solution.py:20
  83.6 5.7 %collective-permute-done.10 = f32[8,2,8,128]{3,2,0,1:T(8,128)S(1)} collective-permute-done((f32[8,2,8,128]{3,2,0,1:T(8,128)S(1)}, f32[8,2,8,128]{3,2,0,1:T(8,128)S(1)}, u32[]{:S(2)}, u32[]{:S(2)}) %collective-permute-start.10) | collective-permute-done | bytes 65568 | tf_op jit(solution)/shard_map/while/body/eval_jaxpr/ppermute | solution.py:20
  89.8 6.0 %collective-permute-done.11 = f32[8,2,8,128]{3,2,0,1:T(8,128)S(1)} collective-permute-done((f32[8,2,8,128]{3,2,0,1:T(8,128)S(1)}, f32[8,2,8,128]{3,2,0,1:T(8,128)S(1)}, u32[]{:S(2)}, u32[]{:S(2)}) %collective-permute-start.11) | collective-permute-done | bytes 65568 | tf_op jit(solution)/shard_map/ppermute | solution.py:20
  96.3 6.3 %collective-permute-done.16 = f32[8,2,8]{2,0,1:T(8,128)S(1)} collective-permute-done((f32[8,2,8]{2,0,1:T(8,128)S(1)}, f32[8,2,8]{2,0,1:T(8,128)S(1)}, u32[]{:S(2)}, u32[]{:S(2)}) %collective-permute-start.16) | collective-permute-done | bytes 544 | tf_op jit(solution)/shard_map/ppermute | solution.py:20
  102.8 8.3 %all_to_all.24 = bf16[4,8,2048]{2,1,0:T(8,128)(2,1)S(1)} all-to-all(bf16[4,8,2048]{2,1,0:T(8,128)(2,1)S(1)} %stack.3), channel_id=1, replica_groups=mesh['groups'=2,'seq'=4,'section'=2,'head'=2] {'seq'}, dimensions={0} | all-to-all | bytes 262144 | tf_op jit(solution)/shard_map/all_to_all | solution.py:144
  111.1 2.2 %convolution_convert_fusion = bf16[32,2048]{1,0:T(8,128)(2,1)} fusion(bf16[2048,2048]{1,0:T(8,128)(2,1)S(1)} %bitcast.95, bf16[4,8,2048]{2,1,0:T(8,128)(2,1)S(1)} %all_to_all.24), kind=kOutput, calls=%fused_computation.8 | convolution fusion | flops 268500992 | bytes 8650752 | tf_op jit(solution)/shard_map/dot_general | solution.py:142
  113.3 0.6 copy.107
  114.0 0.7 copy.110
  114.7 17.2 %reduce-scatter.5.cloned.1.call-done = bf16[8,2048]{1,0:T(8,128)(2,1)} async-done(((bf16[32,2048]{1,0:T(8,128)(2,1)}), bf16[8,2048]{1,0:T(8,128)(2,1)}) %reduce-scatter.5.cloned.1.call-update) | async-done | bytes 32784 | tf_op jit(solution)/shard_map/reduce_scatter | solution.py:149
  (71 shorter events, 5.3 us)
Async XLA Ops:
  7.2 8.7 %copy-start.4 = (s32[64]{0:T(128)S(1)}, s32[64]{0:T(128)}, u32[]{:S(2)}) copy-start(s32[64]{0:T(128)} %param.18) | copy-start | bytes 772
  7.2 8.7 %copy-start.5 = (s32[8]{0:T(128)S(1)}, s32[8]{0:T(128)}, u32[]{:S(2)}) copy-start(s32[8]{0:T(128)} %param.19) | copy-start | bytes 100
  7.2 10.9 %copy-start.3 = (bf16[8,16,128]{2,1,0:T(8,128)(2,1)S(1)}, bf16[8,16,128]{2,1,0:T(8,128)(2,1)}, u32[]{:S(2)}) copy-start(bf16[8,16,128]{2,1,0:T(8,128)(2,1)} %param.10) | copy-start | bytes 98308
  9.5 32.8 %all-to-all-start = ((bf16[64,4,2048]{2,0,1:T(8,128)(2,1)}), bf16[64,4,2048]{2,0,1:T(8,128)(2,1)S(1)}, u32[]{:S(2)}, u32[]{:S(2)}) async-start(bf16[64,4,2048]{2,0,1:T(8,128)(2,1)} %bitcast.92), calls=%async_computation | async-start | bytes 2097152 | tf_op jit(solution)/shard_map/all_to_all | solution.py:112
  15.9 48.6 %reduce-scatter.7.cloned.1.call-start = ((), (), s32[]{:S(2)}) async-start(), calls=%async_computation.5 | async-start | bytes 327680 | tf_op jit(solution)/shard_map/reduce_scatter | solution.py:114
  16.1 30.1 %collective-permute-start.1 = (f32[8]{0:T(128)S(1)}, f32[8]{0:T(128)S(1)}, u32[]{:S(2)}, u32[]{:S(2)}) collective-permute-start(f32[8]{0:T(128)S(1)} %convert_element_type.49), channel_id=1, source_target_pairs={{0,4},{4,8},{8,12},{12,0},{1,5},{5,9},{9,13},{13,1},{2,6},{6,10},{... | collective-permute-start | bytes 104 | tf_op jit(solution)/shard_map/while/body/eval_jaxpr/ppermute | solution.py:20
  18.1 33.4 %collective-permute-start.2 = (bf16[8,16,128]{2,1,0:T(8,128)(2,1)S(1)}, bf16[8,16,128]{2,1,0:T(8,128)(2,1)S(1)}, u32[]{:S(2)}, u32[]{:S(2)}) collective-permute-start(bf16[8,16,128]{2,1,0:T(8,128)(2,1)S(1)} %copy-done.3), channel_id=1, source_target_pairs={{0,4},{4,8},{8,12},{12,0},{1,5},{5,9},{9,13},{13,1},{2,6},{6,10},{... | collective-permute-start | bytes 98312 | tf_op jit(solution)/shard_map/while/body/eval_jaxpr/ppermute | solution.py:20
  42.3 3.3 %copy-start = (bf16[1984,2,128]{2,1,0:T(2,128)(2,1)S(1)}, bf16[1984,2,128]{2,1,0:T(2,128)(2,1)}, u32[]{:S(2)}) copy-start(bf16[1984,2,128]{2,1,0:T(2,128)(2,1)} %param.11) | copy-start | bytes 3047428
  44.7 1.3 copy-start.1
  45.6 86.3 %reduce-scatter.5.cloned.1.call-start = ((), (), s32[]{:S(2)}) async-start(), calls=%async_computation.4 | async-start | bytes 163840 | tf_op jit(solution)/shard_map/reduce_scatter | solution.py:149
  45.6 19.9 %copy-start.2 = (f32[128]{0:T(128)S(1)}, f32[128]{0:T(128)}, u32[]{:S(2)}) copy-start(f32[128]{0:T(128)} %param.16) | copy-start | bytes 1540
  46.1 5.4 %collective-permute-start.4 = (f32[8]{0:T(128)S(1)}, f32[8]{0:T(128)S(1)}, u32[]{:S(2)}, u32[]{:S(2)}) collective-permute-start(f32[8]{0:T(128)S(1)} %collective-permute-done.1), channel_id=1, source_target_pairs={{0,4},{4,8},{8,12},{12,0},{1,5},{5,9},{9,13},{13,1},{2,6},{6,10},{... | collective-permute-start | bytes 104 | tf_op jit(solution)/shard_map/while/body/eval_jaxpr/ppermute | solution.py:20
  51.6 5.4 %collective-permute-start.7 = (f32[8]{0:T(128)S(1)}, f32[8]{0:T(128)S(1)}, u32[]{:S(2)}, u32[]{:S(2)}) collective-permute-start(f32[8]{0:T(128)S(1)} %collective-permute-done.4), channel_id=1, source_target_pairs={{0,4},{4,8},{8,12},{12,0},{1,5},{5,9},{9,13},{13,1},{2,6},{6,10},{... | collective-permute-start | bytes 104 | tf_op jit(solution)/shard_map/ppermute | solution.py:20
  51.6 5.9 %collective-permute-start.5 = (bf16[8,16,128]{2,1,0:T(8,128)(2,1)S(1)}, bf16[8,16,128]{2,1,0:T(8,128)(2,1)S(1)}, u32[]{:S(2)}, u32[]{:S(2)}) collective-permute-start(bf16[8,16,128]{2,1,0:T(8,128)(2,1)S(1)} %collective-permute-done.2), channel_id=1, source_target_pairs={{0,4},{4,8},{8,12},{12,0},{1,5},{5,9},{9,13},{13,1},{2,6},{6,10},{... | collective-permute-start | bytes 98312 | tf_op jit(solution)/shard_map/while/body/eval_jaxpr/ppermute | solution.py:20
  57.5 12.8 %collective-permute-start.8 = (bf16[8,16,128]{2,1,0:T(8,128)(2,1)S(1)}, bf16[8,16,128]{2,1,0:T(8,128)(2,1)S(1)}, u32[]{:S(2)}, u32[]{:S(2)}) collective-permute-start(bf16[8,16,128]{2,1,0:T(8,128)(2,1)S(1)} %collective-permute-done.5), channel_id=1, source_target_pairs={{0,4},{4,8},{8,12},{12,0},{1,5},{5,9},{9,13},{13,1},{2,6},{6,10},{... | collective-permute-start | bytes 98312 | tf_op jit(solution)/shard_map/ppermute | solution.py:20
  66.2 5.5 %collective-permute-start = (f32[8,2,8]{2,0,1:T(8,128)S(1)}, f32[8,2,8]{2,0,1:T(8,128)S(1)}, u32[]{:S(2)}, u32[]{:S(2)}) collective-permute-start(f32[8,2,8]{2,0,1:T(8,128)S(1)} %broadcast_maximum_fusion), channel_id=1, source_target_pairs={{0,4},{4,8},{8,12},{12,0},{1,5},{5,9},{9,13},{13,1},{2,6},{6,10},{... | collective-permute-start | bytes 1544 | tf_op jit(solution)/shard_map/while/body/eval_jaxpr/ppermute | solution.py:20
  67.3 15.4 %collective-permute-start.9 = (f32[8,2,8,128]{3,2,0,1:T(8,128)S(1)}, f32[8,2,8,128]{3,2,0,1:T(8,128)S(1)}, u32[]{:S(2)}, u32[]{:S(2)}) collective-permute-start(f32[8,2,8,128]{3,2,0,1:T(8,128)S(1)} %fusion.14), channel_id=1, source_target_pairs={{0,4},{4,8},{8,12},{12,0},{1,5},{5,9},{9,13},{13,1},{2,6},{6,10},{... | collective-permute-start | bytes 196616 | tf_op jit(solution)/shard_map/while/body/eval_jaxpr/ppermute | solution.py:20
  68.6 5.8 %collective-permute-start.13 = (f32[8,2,8]{2,0,1:T(8,128)S(1)}, f32[8,2,8]{2,0,1:T(8,128)S(1)}, u32[]{:S(2)}, u32[]{:S(2)}) collective-permute-start(f32[8,2,8]{2,0,1:T(8,128)S(1)} %get-tuple-element.67), channel_id=1, source_target_pairs={{0,4},{4,8},{8,12},{12,0},{1,5},{5,9},{9,13},{13,1},{2,6},{6,10},{... | collective-permute-start | bytes 1544 | tf_op jit(solution)/shard_map/while/body/eval_jaxpr/ppermute | solution.py:20
  71.7 5.4 %collective-permute-start.3 = (f32[8,2,8]{2,0,1:T(8,128)S(1)}, f32[8,2,8]{2,0,1:T(8,128)S(1)}, u32[]{:S(2)}, u32[]{:S(2)}) collective-permute-start(f32[8,2,8]{2,0,1:T(8,128)S(1)} %max.22), channel_id=1, source_target_pairs={{0,4},{4,8},{8,12},{12,0},{1,5},{5,9},{9,13},{13,1},{2,6},{6,10},{... | collective-permute-start | bytes 1544 | tf_op jit(solution)/shard_map/while/body/eval_jaxpr/ppermute | solution.py:20
  74.5 5.5 %collective-permute-start.14 = (f32[8,2,8]{2,0,1:T(8,128)S(1)}, f32[8,2,8]{2,0,1:T(8,128)S(1)}, u32[]{:S(2)}, u32[]{:S(2)}) collective-permute-start(f32[8,2,8]{2,0,1:T(8,128)S(1)} %get-tuple-element.58), channel_id=1, source_target_pairs={{0,4},{4,8},{8,12},{12,0},{1,5},{5,9},{9,13},{13,1},{2,6},{6,10},{... | collective-permute-start | bytes 1544 | tf_op jit(solution)/shard_map/while/body/eval_jaxpr/ppermute | solution.py:20
  77.2 5.5 %collective-permute-start.6 = (f32[8,2,8]{2,0,1:T(8,128)S(1)}, f32[8,2,8]{2,0,1:T(8,128)S(1)}, u32[]{:S(2)}, u32[]{:S(2)}) collective-permute-start(f32[8,2,8]{2,0,1:T(8,128)S(1)} %max.23), channel_id=1, source_target_pairs={{0,4},{4,8},{8,12},{12,0},{1,5},{5,9},{9,13},{13,1},{2,6},{6,10},{... | collective-permute-start | bytes 1544 | tf_op jit(solution)/shard_map/ppermute | solution.py:20
  80.0 9.8 %collective-permute-start.15 = (f32[8,2,8]{2,0,1:T(8,128)S(1)}, f32[8,2,8]{2,0,1:T(8,128)S(1)}, u32[]{:S(2)}, u32[]{:S(2)}) collective-permute-start(f32[8,2,8]{2,0,1:T(8,128)S(1)} %get-tuple-element.56), channel_id=1, source_target_pairs={{0,4},{4,8},{8,12},{12,0},{1,5},{5,9},{9,13},{13,1},{2,6},{6,10},{... | collective-permute-start | bytes 1544 | tf_op jit(solution)/shard_map/ppermute | solution.py:20
  83.1 6.1 %collective-permute-start.10 = (f32[8,2,8,128]{3,2,0,1:T(8,128)S(1)}, f32[8,2,8,128]{3,2,0,1:T(8,128)S(1)}, u32[]{:S(2)}, u32[]{:S(2)}) collective-permute-start(f32[8,2,8,128]{3,2,0,1:T(8,128)S(1)} %multiply_add_fusion.2), channel_id=1, source_target_pairs={{0,4},{4,8},{8,12},{12,0},{1,5},{5,9},{9,13},{13,1},{2,6},{6,10},{... | collective-permute-start | bytes 196616 | tf_op jit(solution)/shard_map/while/body/eval_jaxpr/ppermute | solution.py:20
  83.2 27.9 %slice-start = ((s8[8388608]{0:T(1024)(128)(4,1)}), s8[4194304]{0:T(1024)(128)(4,1)S(1)}, s32[]{:S(2)}) async-start(s8[8388608]{0:T(1024)(128)(4,1)} %bitcast.94), calls=%async_computation.6 | async-start | bytes 8388608
  89.2 21.8 %slice-start.1 = ((s8[8388608]{0:T(1024)(128)(4,1)}), s8[4194304]{0:T(1024)(128)(4,1)S(1)}, s32[]{:S(2)}) async-start(s8[8388608]{0:T(1024)(128)(4,1)} %bitcast.94), calls=%async_computation.7 | async-start | bytes 8388608
  89.7 6.1 %collective-permute-start.11 = (f32[8,2,8,128]{3,2,0,1:T(8,128)S(1)}, f32[8,2,8,128]{3,2,0,1:T(8,128)S(1)}, u32[]{:S(2)}, u32[]{:S(2)}) collective-permute-start(f32[8,2,8,128]{3,2,0,1:T(8,128)S(1)} %multiply_add_fusion.1), channel_id=1, source_target_pairs={{0,4},{4,8},{8,12},{12,0},{1,5},{5,9},{9,13},{13,1},{2,6},{6,10},{... | collective-permute-start | bytes 196616 | tf_op jit(solution)/shard_map/ppermute | solution.py:20
  96.2 6.4 %collective-permute-start.12 = (f32[8,2,8,128]{3,2,0,1:T(8,128)S(1)}, f32[8,2,8,128]{3,2,0,1:T(8,128)S(1)}, u32[]{:S(2)}, u32[]{:S(2)}) collective-permute-start(f32[8,2,8,128]{3,2,0,1:T(8,128)S(1)} %multiply_add_fusion), channel_id=1, source_target_pairs={{0,4},{4,8},{8,12},{12,0},{1,5},{5,9},{9,13},{13,1},{2,6},{6,10},{... | collective-permute-start | bytes 196616 | tf_op jit(solution)/shard_map/ppermute | solution.py:20
  96.3 6.4 %collective-permute-start.16 = (f32[8,2,8]{2,0,1:T(8,128)S(1)}, f32[8,2,8]{2,0,1:T(8,128)S(1)}, u32[]{:S(2)}, u32[]{:S(2)}) collective-permute-start(f32[8,2,8]{2,0,1:T(8,128)S(1)} %get-tuple-element.54), channel_id=1, source_target_pairs={{0,4},{4,8},{8,12},{12,0},{1,5},{5,9},{9,13},{13,1},{2,6},{6,10},{... | collective-permute-start | bytes 1544 | tf_op jit(solution)/shard_map/ppermute | solution.py:20
Sparse Core Ops, SparseCore 0:
  45.7 18.7 reduce-scatter.6
  113.4 18.3 reduce-scatter.4
